TPU v7x, 256 devices: a whole 4x4x8 slice. The times are simulated.
256 devices in a mesh: dp: 64 (over y, z_lo, x), ctx: 4 (over z_hi, core).
Axes of the slice: x: 4, y: 4, z: 8 (z_hi: 2, z_lo: 4; z = z_hi * 4 + z_lo), core: 2. Of those that a mesh axis runs over, the one named last changes fastest.
Arguments:
- hidden: bfloat16 [64, 512, 3584], P('dp', 'ctx'), may hold values from -6 to 6
- norm_gain: bfloat16 [3584], replicated, may hold values from 0.099609375 to 1.8984375
- w_query: bfloat16 [3584, 2048], P('dp'), may hold values from -0.09375 to 0.09375
- w_key: bfloat16 [3584, 512], P('dp'), may hold values from -0.09375 to 0.09375
- w_value: bfloat16 [3584, 512], P('dp'), may hold values from -0.09375 to 0.09375
- bias_query: bfloat16 [2048], replicated, may hold values from -4 to 4
- bias_key: bfloat16 [512], replicated, may hold values from -4 to 4
- bias_value: bfloat16 [512], replicated, may hold values from -4 to 4
- kv_blocks: int32 [16, 4, 4], P('ctx'), may hold values from 0 to 3, as said below
- block_counts: int32 [16, 4], P('ctx'), may hold values from 1 to 4, as said below
Outputs:
- attended: bfloat16 [64, 512, 2048], P('dp', 'ctx')
Inputs may be any that keep to these rules, and one draw needn't show every extreme that they name: Entry 0 of kv_blocks[h, b] is b itself; entries 1 to block_counts[h, b] - 1 are distinct blocks below b; later entries are valid block numbers that are not used. block_counts[h, b] is at most b + 1, and the last query block of every head has 4.
All inputs are finite; a program needn't handle non-finite values.
Results may differ from a plain program's by a relative error of at most 0.0053.
Values may be sent and summed in bfloat16 or wider, within the bound.
No kernel may reach another device: no remote copies, remote signals or barrier semaphores. Data moves between devices by JAX's collectives and lax.ppermute only.
A program may use at most 64 MiB of HBM per device.

v0:
```python
import jax
import jax.numpy as jnp
from jax import lax
from jax.sharding import PartitionSpec as P

KVH = 4
HEAD = 128
QHEADS = 16
BLOCK = 128
MAXB = 4
EPSILON = 1e-06
THETA = 1000000.0


def rms_norm(tokens, norm_gain):
    floats = tokens.astype(jnp.float32)
    meansq = jnp.mean(floats * floats, axis=-1, keepdims=True)
    return (floats * lax.rsqrt(meansq + EPSILON) * norm_gain.astype(jnp.float32)).astype(
        jnp.bfloat16
    )


def rotary(heads_in, position):
    half_size = heads_in.shape[-1] // 2
    exponent = jnp.arange(half_size, dtype=jnp.float32) * (2.0 / heads_in.shape[-1])
    inverse = jnp.power(jnp.float32(THETA), -exponent)
    angles = position[:, None] * inverse[None, :]
    cosine = jnp.cos(angles)[:, None, :]
    sine = jnp.sin(angles)[:, None, :]
    first = heads_in[..., :half_size]
    second = heads_in[..., half_size:]
    return jnp.concatenate(
        [first * cosine - second * sine, second * cosine + first * sine], axis=-1
    )


def finish_heads(summed, bias, heads, position, rotate_it):
    shaped = (summed + bias.astype(jnp.float32)).reshape(summed.shape[0], heads, HEAD)
    if rotate_it:
        shaped = rotary(shaped, position)
    return shaped.astype(jnp.bfloat16)


def fold_rows(source, pieces):
    return tuple((jnp.dot(source, piece, preferred_element_type=jnp.float32) for piece in pieces))


def sparse_head(queries, key_rows, value_rows, blocks, counts):
    nblocks = queries.shape[0] // BLOCK
    query_tiles = queries.reshape(nblocks, BLOCK, HEAD)
    key_tiles = key_rows.reshape(nblocks, BLOCK, HEAD)[blocks].reshape(nblocks, MAXB * BLOCK, HEAD)
    value_tiles = value_rows.reshape(nblocks, BLOCK, HEAD)[blocks].reshape(
        nblocks, MAXB * BLOCK, HEAD
    )
    scores = jnp.einsum(
        "qih,qjh->qij", query_tiles, key_tiles, preferred_element_type=jnp.float32
    ) * HEAD ** (-0.5)
    column = jnp.arange(MAXB * BLOCK)
    slot_of = column // BLOCK
    inside = column % BLOCK
    row_pos = jnp.arange(BLOCK)
    allowed = (slot_of[None, None, :] < counts[:, None, None]) & (
        (slot_of[None, None, :] > 0) | (inside[None, None, :] <= row_pos[None, :, None])
    )
    expo = jnp.where(allowed, jnp.exp(scores), jnp.float32(0.0))
    totals = jnp.sum(expo, axis=-1)
    probs = expo.astype(jnp.bfloat16)
    mixed = (
        jnp.einsum("qij,qjh->qih", probs, value_tiles, preferred_element_type=jnp.float32)
        / totals[..., None]
    )
    return mixed.astype(jnp.bfloat16).reshape(nblocks * BLOCK, HEAD)


def one_head(packed):
    return sparse_head(packed[0], packed[1], packed[2], packed[3], packed[4])


def body(
    hidden,
    norm_gain,
    w_query,
    w_key,
    w_value,
    bias_query,
    bias_key,
    bias_value,
    kv_blocks,
    block_counts,
):
    groups = lax.axis_size("ctx")
    device = lax.axis_index("ctx")
    tokens = hidden[0]
    local_rows = tokens.shape[0]
    seq_len = local_rows * groups
    heads_here = QHEADS // groups
    kv_here = KVH // groups
    width_query = heads_here * HEAD
    width_pair = kv_here * HEAD
    normed = rms_norm(tokens, norm_gain)
    sum_query, sum_key, sum_value = fold_rows(
        normed,
        (
            lax.all_gather(w_query, "dp", axis=0, tiled=True),
            lax.all_gather(w_key, "dp", axis=0, tiled=True),
            lax.all_gather(w_value, "dp", axis=0, tiled=True),
        ),
    )
    position = (device * local_rows + jnp.arange(local_rows, dtype=jnp.int32)).astype(jnp.float32)
    queries = finish_heads(sum_query, bias_query, QHEADS, position, True)
    key_rows = finish_heads(sum_key, bias_key, KVH, position, True)
    value_rows = finish_heads(sum_value, bias_value, KVH, position, False)
    query_send = queries.reshape(local_rows, groups, width_query)
    pair_send = jnp.concatenate([key_rows, value_rows], axis=2)
    query_got, pair_got = (
        lax.all_to_all(query_send, "ctx", split_axis=1, concat_axis=0, tiled=True),
        lax.all_to_all(pair_send, "ctx", split_axis=1, concat_axis=0, tiled=True),
    )
    queries = query_got.reshape(seq_len, heads_here, HEAD)
    key_rows = pair_got[:, 0, :width_pair].reshape(seq_len, kv_here, HEAD)
    value_rows = pair_got[:, 0, width_pair:].reshape(seq_len, kv_here, HEAD)
    group = heads_here // kv_here
    key_rows = jnp.repeat(key_rows, group, axis=1)
    value_rows = jnp.repeat(value_rows, group, axis=1)
    mixed = lax.map(
        one_head,
        (
            queries.transpose(1, 0, 2),
            key_rows.transpose(1, 0, 2),
            value_rows.transpose(1, 0, 2),
            kv_blocks,
            block_counts,
        ),
    )
    result = mixed.transpose(1, 0, 2).reshape(seq_len, 1, width_query)
    returned = lax.all_to_all(result, "ctx", split_axis=0, concat_axis=1, tiled=True)
    return returned.reshape(1, local_rows, QHEADS * HEAD)


def solution(mesh):
    placed = (
        P("dp", "ctx", None),
        P(),
        P("dp", None),
        P("dp", None),
        P("dp", None),
        P(),
        P(),
        P(),
        P("ctx", None, None),
        P("ctx", None),
    )
    return jax.shard_map(
        body, mesh=mesh, in_specs=placed, out_specs=P("dp", "ctx", None), check_vma=False
    )
```

profile of v0, /device:TPU:2, one launch (start us, length us, event | category | flops | bytes accessed | tf_op | source)
XLA Modules:
  0.0 1162.7 jit_solution(7236101994991256935)
XLA Ops:
  6.5 0.7 all-gather.8.cloned.1.call-update
  7.3 0.7 all-gather.6.cloned.1.call-update
  8.1 0.7 all-gather.4.cloned.1.call-update
  8.7 0.7 convert_element_type.56
  9.4 0.7 convert_element_type.54
  10.1 0.7 convert_element_type.60
  10.8 0.7 convert_element_type.59
  11.9 1.5 fusion.13
  13.4 350.6 %all-gather.8.cloned.1.call-done = bf16[3584,512]{1,0:T(8,128)(2,1)} async-done(((bf16[56,512]{1,0:T(8,128)(2,1)}), bf16[3584,512]{1,0:T(8,128)(2,1)}) %all-gather.8.cloned.1.call-update) | async-done | bytes 3670032 | tf_op jit(solution)/shard_map/all_gather | solution.py:106
  364.0 3.0 fusion.17
  367.1 349.2 %all-gather.6.cloned.1.call-done = bf16[3584,512]{1,0:T(8,128)(2,1)} async-done(((bf16[56,512]{1,0:T(8,128)(2,1)}), bf16[3584,512]{1,0:T(8,128)(2,1)}) %all-gather.6.cloned.1.call-update) | async-done | bytes 3670032 | tf_op jit(solution)/shard_map/all_gather | solution.py:105
  716.3 2.8 convolution_add_fusion.2
  719.4 0.9 pad_maximum_fusion.1
  720.3 4.1 all-to-all-start.1
  724.4 367.1 %all-gather.4.cloned.1.call-done = bf16[3584,2048]{1,0:T(8,128)(2,1)} async-done(((bf16[56,2048]{1,0:T(8,128)(2,1)}), bf16[3584,2048]{1,0:T(8,128)(2,1)}) %all-gather.4.cloned.1.call-update) | async-done | bytes 14680080 | tf_op jit(solution)/shard_map/all_gather | solution.py:104
  1091.4 7.3 convolution_add_fusion
  1099.3 0.8 pad_maximum_fusion
  1100.1 7.0 all-to-all-start
  1107.1 12.7 %all-to-all-done = bf16[128,4,512]{0,2,1:T(8,128)(2,1)S(1)} async-done(((bf16[128,4,512]{0,2,1:T(8,128)(2,1)}), bf16[128,4,512]{0,2,1:T(8,128)(2,1)S(1)}, u32[]{:S(2)}, u32[]{:S(2)}) %all-to-all-start) | async-done | bytes 524320 | tf_op jit(solution)/shard_map/all_to_all | solution.py:116
  1120.4 0.7 copy-done.1
  1121.1 15.8 %while.12 = (s32[]{:T(128)}, bf16[4,512,128]{1,2,0:T(8,128)(2,1)S(1)}, s32[4,4]{1,0:T(4,128)}, bf16[4,512,128]{2,1,0:T(8,128)(2,1)S(1)}, bf16[4,512,128]{2,1,0:T...) while((s32[]{:T(128)}, bf16[4,512,128]{1,2,0:T(8,128)(2,1)S(1)}, ...), condition=%wide.region_3.4_spmd, body=%wide.region_1.3_spmd.sunk | while | flops 135803952 | bytes 5920353 | solution.py:125
  1121.1 0.7 compare_select_fusion.2
  1123.3 0.7 fusion.45
  1125.0 0.7 compare_select_fusion.2
  1127.3 0.7 fusion.45
  1129.0 0.7 compare_select_fusion.2
  1131.2 0.7 fusion.45
  1133.0 0.7 compare_select_fusion.2
  1135.2 0.7 fusion.45
  1137.4 1.0 reduce
  1139.0 15.2 %all_to_all.48 = bf16[4,2,32768]{2,1,0:T(2,128)(2,1)S(1)} all-to-all(bf16[4,2,32768]{2,1,0:T(2,128)(2,1)S(1)} %reshape.302), channel_id=1, replica_groups=mesh['dp'=64,'ctx'=4] {'ctx'}, dimensions={0} | all-to-all | bytes 1048576 | tf_op jit(solution)/shard_map/all_to_all | solution.py:136
  1155.1 1.0 copy.42
  (88 shorter events, 13.9 us)
Async XLA Ops:
  6.5 357.5 %all-gather.8.cloned.1.call-start = ((), (), s32[]{:S(2)}) async-start(), calls=%async_computation.5 | async-start | bytes 3727360 | tf_op jit(solution)/shard_map/all_gather | solution.py:106
  7.3 709.0 %all-gather.6.cloned.1.call-start = ((), (), s32[]{:S(2)}) async-start(), calls=%async_computation.4 | async-start | bytes 3727360 | tf_op jit(solution)/shard_map/all_gather | solution.py:105
  8.0 1083.4 %all-gather.4.cloned.1.call-start = ((), (), s32[]{:S(2)}) async-start(), calls=%async_computation.3 | async-start | bytes 14909440 | tf_op jit(solution)/shard_map/all_gather | solution.py:104
  13.4 702.9 %copy-start = (bf16[1,128,3584]{2,1,0:T(8,128)(2,1)S(1)}, bf16[1,128,3584]{2,1,0:T(8,128)(2,1)}, u32[]{:S(2)}) copy-start(bf16[1,128,3584]{2,1,0:T(8,128)(2,1)} %param.12) | copy-start | bytes 2752516
  720.3 379.8 %all-to-all-start.1 = ((bf16[128,4,256]{2,0,1:T(8,128)(2,1)}), bf16[128,4,256]{2,0,1:T(8,128)(2,1)S(1)}, u32[]{:S(2)}, u32[]{:S(2)}) async-start(bf16[128,4,256]{2,0,1:T(8,128)(2,1)} %pad_maximum_fusion.1), calls=%async_computation.1 | async-start | bytes 524288 | tf_op jit(solution)/shard_map/all_to_all | solution.py:117
  1100.1 19.7 %all-to-all-start = ((bf16[128,4,512]{0,2,1:T(8,128)(2,1)}), bf16[128,4,512]{0,2,1:T(8,128)(2,1)S(1)}, u32[]{:S(2)}, u32[]{:S(2)}) async-start(bf16[128,4,512]{0,2,1:T(8,128)(2,1)} %bitcast.10), calls=%async_computation | async-start | bytes 1048576 | tf_op jit(solution)/shard_map/all_to_all | solution.py:116
  1120.0 1.0 copy-start.1
Sparse Core Ops, SparseCore 0:
  9.1 354.8 all-gather.7
  365.8 350.3 all-gather.5
  718.0 373.3 all-gather.3
where the time goes:
time: 1160 us
  waiting for transfers between devices  1080 us (93%)
  matrix products  16.3 us (1%)
  blocking collectives  15.2 us (1%)
  local copies, waits for them, and re-layouts  14.1 us (1%)
  between operations  13.3 us (1%)
    all_gather x1, waiting for transfers between devices, body(): lax.all_gather(w_query, 'dp', axis=0, tiled=True)  367 us
    all_gather x1, waiting for transfers between devices, body(): lax.all_gather(w_value, 'dp', axis=0, tiled=True)  351 us
    all_gather x1, waiting for transfers between devices, body(): lax.all_gather(w_key, 'dp', axis=0, tiled=True)  349 us
  transfers between devices with their start and end apart: 5, of which 4 were waited for; matrix products, arithmetic and copies ran while one was open for 2% of the time, Pallas kernels for 0%

commit v1 on v0

--- a/solution.py
+++ b/solution.py
@@ -103,7 +103,9 @@
         (
             lax.all_gather(w_query, "dp", axis=0, tiled=True),
             lax.all_gather(w_key, "dp", axis=0, tiled=True),
-            lax.all_gather(w_value, "dp", axis=0, tiled=True),
+            jnp.concatenate(
+                lax.all_to_all(jnp.stack([w_value] * lax.axis_size("dp")), "dp", 0, 0), axis=0
+            ),
         ),
     )
     position = (device * local_rows + jnp.arange(local_rows, dtype=jnp.int32)).astype(jnp.float32)

time: 1160 us -> 818 us (0.71)
  waiting for transfers between devices: 1080 us -> 726 us
    all_gather x1 -> x0, waiting for transfers between devices: 351 us -> none  [body(): lax.all_gather(w_value, 'dp', axis=0, tiled=True)]
    all_gather x1, waiting for transfers between devices: 349 us -> 251 us  [body(): lax.all_gather(w_key, 'dp', axis=0, tiled=True)]
    all_to_all x0 -> x1, waiting for transfers between devices: none -> 92.9 us  [body(): lax.all_to_all(jnp.stack([w_value] * lax.axis_size('dp')), 'dp', 0, 0)]
    all_to_all x0 -> x1, starting transfers between devices: none -> 12.4 us  [body(): lax.all_to_all(jnp.stack([w_value] * lax.axis_size('dp')), 'dp', 0, 0)]
where the time goes in v1:
time: 818 us; the launch traced here: 815 us
  waiting for transfers between devices  726 us (89%)
  starting transfers between devices  20.4 us (2%)
  local copies, waits for them, and re-layouts  17 us (2%)
  matrix products  15.9 us (2%)
  blocking collectives  15.2 us (2%)
  between operations  13.7 us (2%)
    all_gather x1, waiting for transfers between devices, body(): lax.all_gather(w_query, 'dp', axis=0, tiled=True)  368 us
    all_gather x1, waiting for transfers between devices, body(): lax.all_gather(w_key, 'dp', axis=0, tiled=True)  251 us
    all_to_all x1, waiting for transfers between devices, body(): lax.all_to_all(jnp.stack([w_value] * lax.axis_size('dp')), 'dp', 0, 0)  92.9 us
  transfers between devices with their start and end apart: 5, of which 4 were waited for; matrix products, arithmetic and copies ran while one was open for 2% of the time, Pallas kernels for 0%

profile of v1, /device:TPU:2, one launch (start us, length us, event | category | flops | bytes accessed | tf_op | source)
XLA Modules:
  0.0 815.2 jit_solution(4256833061810522466)
XLA Ops:
  6.5 0.7 all-gather.5.cloned.1.call-update
  7.3 0.7 all-gather.3.cloned.1.call-update
  8.0 2.9 stack.2
  10.9 12.4 %all-to-all-start.1 = ((bf16[64,56,512]{2,1,0:T(8,128)(2,1)}), bf16[64,56,512]{2,1,0:T(8,128)(2,1)}, u32[]{:S(2)}, u32[]{:S(2)}) async-start(bf16[64,56,512]{2,1,0:T(8,128)(2,1)} %stack.2), calls=%async_computation.1 | async-start | bytes 7340032 | tf_op jit(solution)/shard_map/all_to_all | solution.py:107
  24.1 92.9 %all-to-all-done.1 = bf16[64,56,512]{2,1,0:T(8,128)(2,1)} async-done(((bf16[64,56,512]{2,1,0:T(8,128)(2,1)}), bf16[64,56,512]{2,1,0:T(8,128)(2,1)}, u32[]{:S(2)}, u32[]{:S(2)}) %all-to-all-start.1) | async-done | bytes 3670048 | tf_op jit(solution)/shard_map/all_to_all | solution.py:107
  117.0 2.7 fusion.21
  119.8 251.0 %all-gather.5.cloned.1.call-done = bf16[3584,512]{1,0:T(8,128)(2,1)} async-done(((bf16[56,512]{1,0:T(8,128)(2,1)}), bf16[3584,512]{1,0:T(8,128)(2,1)}) %all-gather.5.cloned.1.call-update) | async-done | bytes 3670032 | tf_op jit(solution)/shard_map/all_gather | solution.py:105
  370.9 2.7 convolution_add_fusion.2
  374.0 0.9 pad_maximum_fusion.1
  374.8 3.4 all-to-all-start.2
  378.3 367.8 %all-gather.3.cloned.1.call-done = bf16[3584,2048]{1,0:T(8,128)(2,1)} async-done(((bf16[56,2048]{1,0:T(8,128)(2,1)}), bf16[3584,2048]{1,0:T(8,128)(2,1)}) %all-gather.3.cloned.1.call-update) | async-done | bytes 14680080 | tf_op jit(solution)/shard_map/all_gather | solution.py:104
  746.0 7.3 convolution_add_fusion
  753.8 0.8 pad_maximum_fusion
  754.7 4.6 all-to-all-start
  759.3 12.7 %all-to-all-done = bf16[128,4,512]{0,2,1:T(8,128)(2,1)S(1)} async-done(((bf16[128,4,512]{0,2,1:T(8,128)(2,1)}), bf16[128,4,512]{0,2,1:T(8,128)(2,1)S(1)}, u32[]{:S(2)}, u32[]{:S(2)}) %all-to-all-start) | async-done | bytes 524320 | tf_op jit(solution)/shard_map/all_to_all | solution.py:118
  772.6 0.7 copy-done.1
  773.3 15.8 %while.12 = (s32[]{:T(128)}, bf16[4,512,128]{1,2,0:T(8,128)(2,1)S(1)}, s32[4,4]{1,0:T(4,128)}, bf16[4,512,128]{2,1,0:T(8,128)(2,1)S(1)}, bf16[4,512,128]{2,1,0:T...) while((s32[]{:T(128)}, bf16[4,512,128]{1,2,0:T(8,128)(2,1)S(1)}, ...), condition=%wide.region_3.4_spmd, body=%wide.region_1.3_spmd.sunk | while | flops 135803952 | bytes 5920353 | solution.py:127
  773.3 0.7 compare_select_fusion.2
  774.7 0.6 gather_fusion.1
  775.5 0.7 fusion.52
  777.2 0.7 compare_select_fusion.2
  778.7 0.6 gather_fusion.1
  779.4 0.7 fusion.52
  781.2 0.7 compare_select_fusion.2
  782.7 0.6 gather_fusion.1
  783.4 0.7 fusion.52
  785.2 0.7 compare_select_fusion.2
  786.6 0.6 gather_fusion.1
  787.4 0.7 fusion.52
  789.6 1.0 reduce
  791.2 15.2 %all_to_all.53 = bf16[4,2,32768]{2,1,0:T(2,128)(2,1)S(1)} all-to-all(bf16[4,2,32768]{2,1,0:T(2,128)(2,1)S(1)} %reshape.321), channel_id=1, replica_groups=mesh['dp'=64,'ctx'=4] {'ctx'}, dimensions={0} | all-to-all | bytes 1048576 | tf_op jit(solution)/shard_map/all_to_all | solution.py:138
  807.3 1.0 copy.42
  (96 shorter events, 11.6 us)
Async XLA Ops:
  6.5 364.3 %all-gather.5.cloned.1.call-start = ((), (), s32[]{:S(2)}) async-start(), calls=%async_computation.5 | async-start | bytes 3727360 | tf_op jit(solution)/shard_map/all_gather | solution.py:105
  7.3 738.8 %all-gather.3.cloned.1.call-start = ((), (), s32[]{:S(2)}) async-start(), calls=%async_computation.4 | async-start | bytes 14909440 | tf_op jit(solution)/shard_map/all_gather | solution.py:104
  10.9 12.4 %copy-start.3 = (bf16[2048]{0:T(1024)(128)(2,1)S(1)}, bf16[2048]{0:T(1024)(128)(2,1)}, u32[]{:S(2)}) copy-start(bf16[2048]{0:T(1024)(128)(2,1)} %param.17) | copy-start | bytes 12292
  10.9 12.4 %copy-start.2 = (bf16[3584]{0:T(1024)(128)(2,1)S(1)}, bf16[3584]{0:T(1024)(128)(2,1)}, u32[]{:S(2)}) copy-start(bf16[3584]{0:T(1024)(128)(2,1)} %param.13) | copy-start | bytes 21508
  10.9 12.5 %copy-start.4 = (bf16[512]{0:T(512)(128)(2,1)S(1)}, bf16[512]{0:T(512)(128)(2,1)}, u32[]{:S(2)}) copy-start(bf16[512]{0:T(512)(128)(2,1)} %param.19) | copy-start | bytes 3076
  10.9 12.5 %copy-start.5 = (bf16[512]{0:T(512)(128)(2,1)S(1)}, bf16[512]{0:T(512)(128)(2,1)}, u32[]{:S(2)}) copy-start(bf16[512]{0:T(512)(128)(2,1)} %param.18) | copy-start | bytes 3076
  10.9 12.9 %copy-start = (bf16[1,128,3584]{2,1,0:T(8,128)(2,1)S(1)}, bf16[1,128,3584]{2,1,0:T(8,128)(2,1)}, u32[]{:S(2)}) copy-start(bf16[1,128,3584]{2,1,0:T(8,128)(2,1)} %param.12) | copy-start | bytes 2752516
  10.9 106.1 %all-to-all-start.1 = ((bf16[64,56,512]{2,1,0:T(8,128)(2,1)}), bf16[64,56,512]{2,1,0:T(8,128)(2,1)}, u32[]{:S(2)}, u32[]{:S(2)}) async-start(bf16[64,56,512]{2,1,0:T(8,128)(2,1)} %stack.2), calls=%async_computation.1 | async-start | bytes 7340032 | tf_op jit(solution)/shard_map/all_to_all | solution.py:107
  374.8 379.8 %all-to-all-start.2 = ((bf16[128,4,256]{2,0,1:T(8,128)(2,1)}), bf16[128,4,256]{2,0,1:T(8,128)(2,1)S(1)}, u32[]{:S(2)}, u32[]{:S(2)}) async-start(bf16[128,4,256]{2,0,1:T(8,128)(2,1)} %pad_maximum_fusion.1), calls=%async_computation.2 | async-start | bytes 524288 | tf_op jit(solution)/shard_map/all_to_all | solution.py:119
  754.7 17.3 %all-to-all-start = ((bf16[128,4,512]{0,2,1:T(8,128)(2,1)}), bf16[128,4,512]{0,2,1:T(8,128)(2,1)S(1)}, u32[]{:S(2)}, u32[]{:S(2)}) async-start(bf16[128,4,512]{0,2,1:T(8,128)(2,1)} %bitcast.9), calls=%async_computation | async-start | bytes 1048576 | tf_op jit(solution)/shard_map/all_to_all | solution.py:118
  772.2 1.0 copy-start.1
Sparse Core Ops, SparseCore 0:
  9.1 361.6 all-gather.4
  372.6 373.3 all-gather.2
